TPU v7x, 256 devices: a whole 4x4x8 slice. The times are simulated.
256 devices in a mesh: head: 16 (over y_hi, z), ctx: 16 (over x, y_lo, core).
Axes of the slice: x: 4, y: 4 (y_hi: 2, y_lo: 2; y = y_hi * 2 + y_lo), z: 8, core: 2. Of those that a mesh axis runs over, the one named last changes fastest.
Arguments:
- queries: bfloat16 [8192, 2048], P(('ctx', 'head')), may hold values from -9 to 9
- keys: bfloat16 [8192, 8192], P('ctx', 'head'), may hold values from -9 to 9
- values: bfloat16 [8192, 8192], P('ctx', 'head'), may hold values from -6 to 6
- routes: int32 [8192, 16], P(('ctx', 'head')), may hold values from 0 to 63, all different within a row; in each aligned block of 32 rows (0 to 31, 32 to 63, ...) at most 16 rows name the same one
- gates: float32 [8192, 16], P(('ctx', 'head')), may hold values from 0.25 to 1
- block_mask: int32 [64, 64], replicated, may hold values 0 or 1
- w_out: bfloat16 [8192, 8192], P('head'), may hold values from -0.125 to 0.125
Outputs:
- mixed: bfloat16 [8192, 8192], P(('ctx', 'head'))
Inputs may be any that keep to these rules, and one draw needn't show every extreme that they name: `routes`: in each aligned block of 32 rows (the rows of one device) no head is named more than 16 times; each row names 16 different heads.
All inputs are finite; a program needn't handle non-finite values.
Results may differ from a plain program's by a relative error of at most 0.015.
Values may be sent and summed in bfloat16 or wider, within the bound.
No kernel may reach another device: no remote copies, remote signals or barrier semaphores. Data moves between devices by JAX's collectives and lax.ppermute only.
A program may use at most 128 MiB of HBM per device.

v0:
```python
import math

import jax
import jax.numpy as jnp
from jax import lax
from jax.sharding import PartitionSpec as P

H = 64
HD = 128
BLK = 128
CAP = 16


def local(queries, keys, values, routes, gates, block_mask, w_out):
    tok_dev, routed = routes.shape
    ctx_tok = keys.shape[0]
    per_dev = keys.shape[1] // HD
    head_count = lax.axis_size("head")
    ctx_count = lax.axis_size("ctx")
    seq_len = ctx_tok * ctx_count
    slot_count = head_count * CAP
    head_ids = jnp.arange(H, dtype=jnp.int32)
    onehot = (routes[:, :, None] == head_ids[None, None, :]).astype(jnp.int32)
    per_token = jnp.sum(onehot, axis=1)
    earlier = jnp.cumsum(per_token, axis=0) - per_token
    ranking = jnp.sum(onehot * earlier[:, None, :], axis=2)
    target = (routes * CAP + ranking).reshape(-1)
    select = (jnp.arange(H * CAP, dtype=jnp.int32)[:, None] == target[None, :]).astype(jnp.bfloat16)
    packed = jnp.dot(
        select, queries.reshape(tok_dev * routed, HD), preferred_element_type=jnp.float32
    ).astype(jnp.bfloat16)
    packed = packed.reshape(head_count, per_dev, CAP, HD)
    arrived = lax.all_to_all(packed, "head", split_axis=0, concat_axis=2, tiled=True).reshape(
        per_dev, slot_count, HD
    )
    group_routes, group_gates = (
        lax.all_gather(routes, "head", axis=0, tiled=True),
        lax.all_gather(gates, "head", axis=0, tiled=True),
    )
    own_heads = lax.axis_index("head") * per_dev + jnp.arange(per_dev, dtype=jnp.int32)
    chosen = (group_routes[:, :, None] == own_heads[None, None, :]).astype(jnp.int32)
    token_hit = jnp.sum(chosen, axis=1)
    token_gate = jnp.sum(chosen.astype(jnp.float32) * group_gates[:, :, None], axis=1)
    block_hit = token_hit.reshape(head_count, tok_dev, per_dev)
    block_rank = jnp.cumsum(block_hit, axis=1) - block_hit
    placed = block_hit[..., None] * (
        block_rank[..., None] == jnp.arange(CAP, dtype=jnp.int32)
    ).astype(jnp.int32)
    diagonal = jnp.eye(head_count, dtype=jnp.int32)
    mapping = placed.transpose(2, 0, 1, 3)[:, :, :, None, :] * diagonal[None, :, None, :, None]
    mapping = mapping.reshape(per_dev, ctx_tok, slot_count)
    slot_token = jnp.sum(mapping * jnp.arange(ctx_tok, dtype=jnp.int32)[None, :, None], axis=1)
    slot_gate = jnp.sum(mapping.astype(jnp.float32) * token_gate.T[:, :, None], axis=1)
    ctx_index = lax.axis_index("ctx")
    query_pos = ctx_index * ctx_tok + slot_token
    blocks = seq_len // BLK
    block_ids = jnp.arange(blocks, dtype=jnp.int32)
    usable = (block_ids[None, :] < block_ids[:, None]) & (block_mask == 1) | (
        block_ids[None, :] == block_ids[:, None]
    )
    query_rows = usable[query_pos // BLK]
    score_scale = 1.0 / math.sqrt(HD)
    start_state = (
        jnp.full((per_dev, slot_count), -1e30, jnp.float32),
        jnp.zeros((per_dev, slot_count), jnp.float32),
        jnp.zeros((per_dev, slot_count, HD), jnp.float32),
    )

    def update(carried, key_block, value_block, key_pos):
        allowed = jnp.take(query_rows, key_pos // BLK, axis=2) & (
            key_pos[None, None, :] <= query_pos[:, :, None]
        )
        peak, total, summed = carried
        scores = (
            jnp.einsum("pqd,kpd->pqk", arrived, key_block, preferred_element_type=jnp.float32)
            * score_scale
        )
        masked = jnp.where(allowed, scores, -1e30)
        new_peak = jnp.maximum(peak, jnp.max(masked, axis=2))
        factor = jnp.exp(peak - new_peak)
        weights = jnp.where(allowed, jnp.exp(scores - new_peak[..., None]), 0.0)
        total = total * factor + jnp.sum(weights, axis=2)
        summed = summed * factor[..., None] + jnp.einsum(
            "pqk,kpd->pqd",
            weights.astype(jnp.bfloat16),
            value_block,
            preferred_element_type=jnp.float32,
        )
        return (new_peak, total, summed)

    key_value = jnp.stack((keys, values))
    piece_pair = lax.all_gather(key_value, "ctx", axis=1, tiled=True)
    length = piece_pair.shape[1]
    block_len = 512
    reshaped = piece_pair.reshape(2, length, per_dev, HD)

    def sub_block(index, current):
        window = lax.dynamic_slice_in_dim(reshaped, index * block_len, block_len, 1)
        key_pos = index * block_len + jnp.arange(block_len, dtype=jnp.int32)
        return update(current, window[0], window[1], key_pos)

    carried = lax.fori_loop(0, length // block_len, sub_block, start_state)
    peak, total, summed = carried
    attended = (summed / total[..., None] * slot_gate[..., None]).astype(jnp.bfloat16)
    weighted = jnp.einsum(
        "ptq,pqd->tpd", mapping.astype(jnp.bfloat16), attended, preferred_element_type=jnp.float32
    )
    weighted = weighted.astype(jnp.bfloat16).reshape(ctx_tok, per_dev * HD)
    return lax.psum_scatter(
        jnp.dot(weighted, w_out, preferred_element_type=jnp.float32).astype(jnp.bfloat16),
        "head",
        scatter_dimension=0,
        tiled=True,
    )


def solution(mesh):
    placed = (
        P(("ctx", "head"), None),
        P("ctx", "head"),
        P("ctx", "head"),
        P(("ctx", "head"), None),
        P(("ctx", "head"), None),
        P(),
        P("head", None),
    )
    return jax.shard_map(
        local, mesh=mesh, in_specs=placed, out_specs=P(("ctx", "head"), None), check_vma=False
    )
```

profile of v0, /device:TPU:4, one launch (start us, length us, event | category | flops | bytes accessed | tf_op | source)
XLA Modules:
  0.0 526.7 jit_solution(619784373170647085)
XLA Ops:
  12.7 11.2 %all-to-all-start = ((bf16[16,4,16,128]{3,2,1,0:T(8,128)(2,1)}), bf16[16,4,16,128]{3,2,1,0:T(8,128)(2,1)S(1)}, u32[]{:S(2)}, u32[]{:S(2)}) async-start(bf16[16,4,16,128]{3,2,1,0:T(8,128)(2,1)} %bitcast.7), calls=%async_computation | async-start | bytes 524288 | tf_op jit(solution)/shard_map/all_to_all | solution.py:33
  24.0 41.7 %all-gather.1 = f32[16,32,16]{1,2,0:T(8,128)S(1)} all-gather(f32[1,32,16]{1,2,0:T(8,128)S(1)} %bitcast.106), channel_id=1, replica_groups=mesh['head'=16,'ctx'=16] {'head'}, dimensions={0}, use_global_device_ids=true | all-gather | bytes 34816 | tf_op jit(solution)/shard_map/all_gather | solution.py:38
  65.9 36.2 %all-gather = s32[16,32,16]{1,2,0:T(8,128)S(1)} all-gather(s32[1,32,16]{1,2,0:T(8,128)S(1)} %bitcast.103), channel_id=1, replica_groups=mesh['head'=16,'ctx'=16] {'head'}, dimensions={0}, use_global_device_ids=true | all-gather | bytes 34816 | tf_op jit(solution)/shard_map/all_gather | solution.py:37
  105.2 18.5 %fusion.18 = s32[4,16,16]{2,1,0:T(8,128)S(1)} fusion(s32[16,32]{1,0:T(8,128)S(1)} %multiply_add_fusion.1, s32[16,16]{0,1:T(8,128)S(1)} %fusion.33, s32[4,16,32,16]{2,1,3,0:T(8,128)S(1)} %fusion.26), kind=kLoop, calls=%fused_computation.47 | loop fusion | flops 1571840 | bytes 138240 | tf_op jit(solution)/shard_map/reduce_sum | solution.py:52
  123.7 3.1 fusion.20
  127.1 3.0 gather_fusion.1
  131.4 4.2 mul.165
  135.6 6.2 %mul.185 = s32[4,512,256]{1,2,0:T(8,128)S(1)} reshape(s32[4,16,32,16,16]{2,1,4,3,0:T(8,128)} %mul.165) | data formatting | bytes 4194304 | tf_op jit(solution)/shard_map/mul | solution.py:50
  142.6 143.2 %while.20 = (s32[]{:T(128)}, f32[4,256]{1,0:T(4,128)S(1)}, f32[4,256]{1,0:T(4,128)S(1)}, f32[4,256,128]{2,1,0:T(8,128)}, pred[4,256,64]{1,0,2:T(4,128)(4,1)S(1)}...) while((s32[]{:T(128)}, f32[4,256]{1,0:T(4,128)S(1)}, ...), condition=%wide.region_9.10_spmd.clone, body=%wide.region_6.9_spmd.clone.sunk | while | flops 279342080 | bytes 11370723 | solution.py:102
  142.7 2.6 gather_fusion
  148.3 3.1 convolution_add_fusion.2
  151.5 2.6 gather_fusion
  157.1 3.2 convolution_add_fusion.2
  160.4 2.6 gather_fusion
  166.1 3.2 convolution_add_fusion.2
  169.4 2.6 gather_fusion
  175.0 3.2 convolution_add_fusion.2
  178.3 2.6 gather_fusion
  184.0 3.2 convolution_add_fusion.2
  192.9 3.2 convolution_add_fusion.2
  201.9 3.2 convolution_add_fusion.2
  210.9 3.2 convolution_add_fusion.2
  219.8 3.2 convolution_add_fusion.2
  228.8 3.2 convolution_add_fusion.2
  237.7 3.2 convolution_add_fusion.2
  246.7 3.2 convolution_add_fusion.2
  255.7 3.2 convolution_add_fusion.2
  264.6 3.2 convolution_add_fusion.2
  273.6 3.2 convolution_add_fusion.2
  282.5 3.2 convolution_add_fusion.2
  287.5 10.1 %convolution_convert_fusion = bf16[512,8192]{1,0:T(8,128)(2,1)} fusion(bf16[512,512]{0,1:T(8,128)(2,1)S(1)} %bitcast.95, bf16[512,8192]{1,0:T(8,128)(2,1)} %param.15), kind=kOutput, calls=%fused_computation.46 | convolution fusion | flops 4299161600 | bytes 17301504 | tf_op jit(solution)/shard_map/dot_general | solution.py:110
  297.7 222.2 %reduce-scatter.2.cloned.1.call-done = bf16[32,8192]{1,0:T(8,128)(2,1)} async-done(((bf16[512,8192]{1,0:T(8,128)(2,1)}), bf16[32,8192]{1,0:T(8,128)(2,1)}) %reduce-scatter.2.cloned.1.call-update) | async-done | bytes 524304 | tf_op jit(solution)/shard_map/reduce_scatter | solution.py:109
  (212 shorter events, 91.2 us)
Async XLA Ops:
  6.5 136.1 %all-gather.4.cloned.1.call-start = ((), (), s32[]{:S(2)}) async-start(), calls=%async_computation.2 | async-start | bytes 17825792 | tf_op jit(solution)/shard_map/all_gather | solution.py:92
  7.8 2.5 copy-start.1
  7.8 3.6 copy-start
  9.1 14.8 %copy-start.3 = (f32[32,16]{0,1:T(8,128)S(1)}, f32[32,16]{0,1:T(8,128)}, u32[]{:S(2)}) copy-start(f32[32,16]{0,1:T(8,128)} %param.13) | copy-start | bytes 6148
  12.7 129.2 %all-to-all-start = ((bf16[16,4,16,128]{3,2,1,0:T(8,128)(2,1)}), bf16[16,4,16,128]{3,2,1,0:T(8,128)(2,1)S(1)}, u32[]{:S(2)}, u32[]{:S(2)}) async-start(bf16[16,4,16,128]{3,2,1,0:T(8,128)(2,1)} %bitcast.7), calls=%async_computation | async-start | bytes 524288 | tf_op jit(solution)/shard_map/all_to_all | solution.py:33
  23.9 495.9 %reduce-scatter.2.cloned.1.call-start = ((), (), s32[]{:S(2)}) async-start(), calls=%async_computation.3 | async-start | bytes 8912896 | tf_op jit(solution)/shard_map/reduce_scatter | solution.py:109
  65.9 61.2 %copy-start.2 = (s32[64,64]{1,0:T(8,128)S(1)}, s32[64,64]{1,0:T(8,128)}, u32[]{:S(2)}) copy-start(s32[64,64]{1,0:T(8,128)} %param.14) | copy-start | bytes 49156
Sparse Core Ops, SparseCore 0:
  10.4 96.5 all-gather.3
  297.8 221.9 reduce-scatter.1
where the time goes:
time: 528 us; the launch traced here: 527 us
  waiting for transfers between devices  222 us (42%)
  matrix products  98.9 us (19%)
  blocking collectives  78 us (15%)
  local copies, waits for them, and re-layouts  60.5 us (11%)
  other arithmetic  41.5 us (8%)
  between operations  13.6 us (3%)
  starting transfers between devices  11.2 us (2%)
    reduce_scatter x1, waiting for transfers between devices, local(): lax.psum_scatter(jnp.dot(weighted, w_out, preferred_element_type=jnp.floa...  222 us
    dot_general x16, matrix products, update(): jnp.einsum('pqk,kpd->pqd', weights.astype(jnp.bfloat16), value_block, pre...  51.7 us
    all_gather x1, blocking collectives, local(): lax.all_gather(gates, 'head', axis=0, tiled=True)  41.7 us
    gather x16, local copies, waits for them, and re-layouts, update(): jnp.take(query_rows, key_pos // BLK, axis=2)  41.1 us
    all_gather x1, blocking collectives, local(): lax.all_gather(routes, 'head', axis=0, tiled=True)  36.2 us
    dot_general x16, matrix products, update(): jnp.einsum('pqd,kpd->pqk', arrived, key_block, preferred_element_type=jnp...  34.1 us
    reduce_sum x1, other arithmetic, local(): jnp.sum(mapping * jnp.arange(ctx_tok, dtype=jnp.int32)[None, :, None], ax...  18.5 us
    reduce_sum x16, other arithmetic, update(): total = total * factor + jnp.sum(weights, axis=2)  14.4 us
  transfers between devices with their start and end apart: 3, of which 1 were waited for; matrix products, arithmetic and copies ran while one was open for 8% of the time, Pallas kernels for 0%

commit v1 on v0

v1 whole, which is shorter than its diff:
```python
import math

import jax
import jax.numpy as jnp
from jax import lax
from jax.experimental import pallas as pl
from jax.experimental.pallas import tpu as pltpu
from jax.sharding import PartitionSpec as P

H = 64
HD = 128
BLK = 128
CAP = 16
NX = 4
NJ = 4
NZ = 8
HALF = 2048
NEG = -1e30
SCALE2 = math.log2(math.e) / math.sqrt(HD)
BF = jnp.bfloat16
F32 = jnp.float32
NT = (((1,), (1,)), ((), ()))


def vmem():
    return pl.BlockSpec(memory_space=pltpu.VMEM)


def grant(mib):
    return pltpu.CompilerParams(vmem_limit_bytes=mib << 20)


def pack_kernel(q_ref, tgt_ref, gate_ref, out_ref):
    rows = jnp.concatenate([q_ref[:, k * HD : (k + 1) * HD] for k in range(16)], axis=0)
    tgt = tgt_ref[...]
    gate = gate_ref[...]
    hi = gate.astype(BF).astype(F32)
    mid = (gate - hi).astype(BF).astype(F32)
    tok = (lax.broadcasted_iota(jnp.int32, (1, 512), 1) % 32 + 1).astype(F32)
    aux = jnp.concatenate([tok, hi, mid, gate - hi - mid, jnp.zeros((12, 512), F32)], axis=0).astype(BF)
    for dest in range(16):
        slot = lax.broadcasted_iota(jnp.int32, (64, 512), 0) + dest * 64
        sel = jnp.where(slot == tgt, 1.0, 0.0).astype(BF)
        out_ref[dest, 0:64, :] = jnp.dot(sel, rows, preferred_element_type=F32).astype(BF)
        meta = lax.dot_general(aux, sel, NT, preferred_element_type=F32)
        meta = jnp.concatenate([meta, jnp.zeros((16, 64), F32)], axis=1)
        out_ref[dest, 64:80, :] = meta.astype(BF)


def attend_kernel(sets, flag_ref, bias_ref, lim_ref, *refs):
    count = len(sets)
    q_refs, kv_refs, out_refs = refs[:count], refs[count : count + 4], refs[count + 4 : 2 * count + 4]
    kv, sems, list_ref, done_ref, s_ref, m_ref, acc_ref = refs[2 * count + 4 :]
    copies = [pltpu.make_async_copy(src, kv.at[i], sems.at[i]) for i, src in enumerate(kv_refs)]
    for copy in copies:
        copy.start()
    copies[0].wait()
    done_ref[0] = jnp.int32(0)

    def keys_ready(last):
        for i in range(1, 4):

            @pl.when((last >= i) & (done_ref[0] < i))
            def _():
                copies[i].wait()
                done_ref[0] = jnp.int32(i)

    ones = jnp.ones((16, 256), BF)
    key_id = lax.broadcasted_iota(jnp.int32, (BLK, 256), 0).astype(F32)

    def two_blocks(q_ref, first, second, bias, lims):
        blocks = (first, second)
        state = {}

        def scores(p):
            q = q_ref[:, p * CAP : (p + 1) * CAP, :].reshape(256, HD)
            old = m_ref[p : p + 1, :]
            new = old
            for n, block in enumerate(blocks):
                k = kv[block // 4, pl.ds(pl.multiple_of((block % 4) * BLK, BLK), BLK), p * HD : (p + 1) * HD]
                s = lax.dot_general(k, q, NT, preferred_element_type=F32)
                if lims is not None:
                    s = jnp.where(key_id <= lims(p, n), s, 2.0 * NEG)
                s_ref[p, n * BLK : (n + 1) * BLK, :] = s
                top = jnp.max(s, axis=0, keepdims=True)
                new = jnp.maximum(new, top if bias is None else top + bias[n])
            m_ref[p : p + 1, :] = new
            state[p] = (new, jnp.exp2((old - new) * SCALE2))

        def values(p):
            new, factor = state[p]
            ws, vts = [], []
            for n, block in enumerate(blocks):
                base = new if bias is None else new - bias[n]
                ws.append(jnp.exp2((s_ref[p, n * BLK : (n + 1) * BLK, :] - base) * SCALE2).astype(BF))
                vts.append(kv[block // 4, 512 + p * HD : 512 + (p + 1) * HD, pl.ds(pl.multiple_of((block % 4) * BLK, BLK), BLK)])
            left = jnp.concatenate([jnp.concatenate(vts, axis=1), ones], axis=0)
            gain = jnp.dot(left, jnp.concatenate(ws, axis=0), preferred_element_type=F32)
            acc_ref[p * 144 : (p + 1) * 144, :] = acc_ref[p * 144 : (p + 1) * 144, :] * factor + gain

        scores(0)
        scores(1)
        values(0)
        scores(2)
        values(1)
        scores(3)
        values(2)
        values(3)

    for n, dx in enumerate(sets):
        q_ref, out_ref = q_refs[n], out_refs[n]
        m_ref[...] = jnp.full(m_ref.shape, NEG, F32)
        acc_ref[...] = jnp.zeros(acc_ref.shape, F32)
        if dx == 0:

            def diag_step(pair, _, q_ref=q_ref):
                def lims(p, n):
                    return lim_ref[pl.ds(p * 4 + pair * 2 + n, 1), :]

                two_blocks(q_ref, pair * 2, pair * 2 + 1, None, lims)
                return 0

            lax.fori_loop(0, 2, diag_step, 0)
        found = jnp.int32(0)
        for block in range(4 if dx == 0 else 0, 16):
            list_ref[found] = jnp.int32(block)
            found = found + flag_ref[dx, block]
        list_ref[found] = jnp.int32(16)

        def pair_step(pair, _, q_ref=q_ref, dx=dx, n=n):
            one, two = list_ref[pair * 2], list_ref[pair * 2 + 1]
            if n == 0:
                keys_ready(jnp.minimum(two, 15) // 4)
            bias = (bias_ref[pl.ds(dx * 24 + one, 1), :], bias_ref[pl.ds(dx * 24 + two, 1), :])
            two_blocks(q_ref, one, jnp.minimum(two, 15), bias, None)
            return 0

        lax.fori_loop(0, (found + 1) // 2, pair_step, 0)
        if n == 0:
            keys_ready(3)
        total = jnp.concatenate([acc_ref[p * 144 + HD : p * 144 + HD + 1, :] for p in range(4)], axis=0)
        some = total > 0.0
        safe = jnp.where(some, total, 1.0)
        inv = jnp.where(some, 1.0 / safe, 0.0)
        lse = jnp.where(some, m_ref[0:4, :] * SCALE2 + jnp.log2(safe), NEG)
        hi = lse.astype(BF)
        rest = lse - hi.astype(F32)
        mid = rest.astype(BF)
        low = (rest - mid.astype(F32)).astype(BF)
        for p in range(4):
            out_ref[p * HD : (p + 1) * HD, :] = (acc_ref[p * 144 : p * 144 + HD, :] * inv[p : p + 1, :]).astype(BF)
        out_ref[512:528, :] = jnp.concatenate([hi, mid, low, jnp.zeros((4, 256), BF)], axis=0)


def attend(sets, flags, bias, lim, qs, kvs):
    part = jax.ShapeDtypeStruct((528, 256), BF)
    return pl.pallas_call(
        lambda *refs: attend_kernel(sets, *refs),
        out_shape=[part] * len(sets),
        in_specs=[pl.BlockSpec(memory_space=pltpu.SMEM)]
        + [vmem()] * (2 + len(sets))
        + [pl.BlockSpec(memory_space=pl.ANY)] * 4,
        out_specs=[vmem()] * len(sets),
        scratch_shapes=[
            pltpu.VMEM((4, 1024, 512), BF),
            pltpu.SemaphoreType.DMA((4,)),
            pltpu.SMEM((18,), jnp.int32),
            pltpu.SMEM((1,), jnp.int32),
            pltpu.VMEM((4, 256, 256), F32),
            pltpu.VMEM((8, 256), F32),
            pltpu.VMEM((576, 256), F32),
        ],
        cost_estimate=pl.CostEstimate(
            flops=len(sets) * 2 * 2 * 4 * 256 * 2048 * 128,
            bytes_accessed=5 << 20,
            transcendentals=len(sets) * 4 * 256 * 2048,
        ),
        compiler_params=grant(24),
        name="attend",
    )(flags, bias, lim, *qs, *kvs)


def place_heads(heads, pos, out_ref, lo):
    token = lax.broadcasted_iota(jnp.int32, (256, HD), 0).astype(F32)
    for r in range(2):
        place = jnp.where(token + r * 256.0 == pos[:, r * HD : (r + 1) * HD], 1.0, 0.0).astype(BF)
        out_ref[r * 256 : (r + 1) * 256, lo : lo + HD] = lax.dot_general(
            place, heads[:, r * HD : (r + 1) * HD], NT, preferred_element_type=F32
        ).astype(BF)


def slot_pos(tok):
    dev = (lax.broadcasted_iota(jnp.int32, tok.shape, 1) // CAP).astype(F32)
    return jnp.where(tok >= 0.0, dev * 32.0 + tok, -1.0)


def merge_kernel(a_ref, b_ref, c_ref, d_ref, tok_ref, gate_ref, send_ref):
    parts = (a_ref, b_ref, c_ref, d_ref)
    lses = []
    for ref in parts:
        tail = ref[512:528, :].astype(F32)
        lses.append(tail[0:4] + tail[4:8] + tail[8:12])
    top = jnp.maximum(jnp.maximum(lses[0], lses[1]), jnp.maximum(lses[2], lses[3]))
    ws = [jnp.exp2(lse - top) for lse in lses]
    norm = gate_ref[...] / (ws[0] + ws[1] + ws[2] + ws[3])
    ws = [w * norm for w in ws]
    for p in range(4):
        mix = None
        for ref, w in zip(parts, ws):
            term = ref[p * HD : (p + 1) * HD, :].astype(F32) * w[p : p + 1, :]
            mix = term if mix is None else mix + term
        send_ref[p * HD : (p + 1) * HD, :] = mix.astype(BF)
    send_ref[512:528, :] = jnp.concatenate([tok_ref[...], jnp.zeros((12, 256), F32)], axis=0).astype(BF)


def own_kernel(place_ref, sent_ref, w_ref, out_ref, a_ref):
    @pl.when(pl.program_id(0) == 0)
    def _():
        pos = slot_pos(sent_ref[512:528, :].astype(F32))
        for p in range(4):
            place_heads(sent_ref[p * HD : (p + 1) * HD, :], pos[p : p + 1, :], a_ref, p * HD)

    out_ref[...] = jnp.dot(a_ref[...], w_ref[...], preferred_element_type=F32).astype(BF)


def partner_kernel(place_ref, got_ref, own_ref, wb_ref, wc_ref, out_ref, plus_ref, minus_ref, a_ref):
    @pl.when(pl.program_id(0) == 0)
    def _():
        pos = slot_pos(got_ref[512:528, :].astype(F32))
        core = place_ref[1]
        for n in range(4):
            half = core if n < 2 else 1 - core
            q = n % 2
            start = pl.multiple_of(half * 256 + q * HD, HD)
            row = jnp.where(half == 0, pos[q : q + 1, :], pos[2 + q : 3 + q, :])
            place_heads(got_ref[pl.ds(start, HD), :], row, a_ref, n * HD)

    total = own_ref[...].astype(F32)
    total += jnp.dot(a_ref[:, 0:256], wb_ref[...], preferred_element_type=F32)
    total += jnp.dot(a_ref[:, 256:512], wc_ref[...], preferred_element_type=F32)
    out_ref[...] = total.astype(BF)
    for ref, dest in ((plus_ref, place_ref[2]), (minus_ref, place_ref[3])):
        for half in range(2):
            ref[half] = out_ref[pl.ds(pl.multiple_of(half * 256 + dest * 32, 32), 32), :]


TILE = 512
STEPS = HALF // TILE


def own_product(place, sent, w_out):
    return pl.pallas_call(
        own_kernel,
        out_shape=jax.ShapeDtypeStruct((512, 2 * HALF), BF),
        grid_spec=pltpu.PrefetchScalarGridSpec(
            num_scalar_prefetch=1,
            grid=(2 * STEPS,),
            in_specs=[
                pl.BlockSpec((528, 256), lambda i, s: (0, 0)),
                pl.BlockSpec((512, TILE), lambda i, s: (0, s[0] * (2 * STEPS) + i)),
            ],
            out_specs=pl.BlockSpec((512, TILE), lambda i, s: (0, i)),
            scratch_shapes=[pltpu.VMEM((512, 512), BF)],
        ),
        cost_estimate=pl.CostEstimate(flops=2 * 512 * 512 * 2 * HALF, bytes_accessed=8 << 20, transcendentals=0),
        name="own_product",
    )(place, sent, w_out)


def with_partner(place, chunk, got, own, wb, wc):
    message = jax.ShapeDtypeStruct((2, 32, HALF), BF)
    return pl.pallas_call(
        partner_kernel,
        out_shape=[jax.ShapeDtypeStruct((512, HALF), BF), message, message],
        grid_spec=pltpu.PrefetchScalarGridSpec(
            num_scalar_prefetch=1,
            grid=(STEPS,),
            in_specs=[
                pl.BlockSpec((528, 256), lambda i, s: (0, 0)),
                pl.BlockSpec((512, TILE), lambda i, s: (0, chunk * STEPS + i)),
                pl.BlockSpec((256, TILE), lambda i, s: (0, i)),
                pl.BlockSpec((256, TILE), lambda i, s: (0, i)),
            ],
            out_specs=[pl.BlockSpec((512, TILE), lambda i, s: (0, i))]
            + [pl.BlockSpec((2, 32, TILE), lambda i, s: (0, 0, i))] * 2,
            scratch_shapes=[pltpu.VMEM((512, 512), BF)],
        ),
        cost_estimate=pl.CostEstimate(flops=2 * 512 * 512 * HALF, bytes_accessed=6 << 20, transcendentals=0),
        name="with_partner",
    )(place, got, own, wb, wc)


def layer(queries, keys, values, routes, gates, block_mask, w_out):
    ctx = lax.axis_index("ctx")
    head = lax.axis_index("head")
    x, j = ctx // NJ, ctx % NJ
    y, z = head // NZ, head % NZ

    def move_ctx(v, f):
        return lax.ppermute(v, "ctx", [(i, f(i)) for i in range(16)])

    def move_head(v, f):
        return lax.ppermute(v, "head", [(i, f(i)) for i in range(16)])

    def swap(i):
        return i ^ NZ

    given = lax.dynamic_slice(w_out, ((ctx % 2) * 256, (1 - y) * 2 * HALF), (256, 2 * HALF))
    w_fetched = [move_head(given[:, n * HALF : (n + 1) * HALF], swap) for n in range(2)]

    kv = jnp.concatenate([keys, values.T], axis=0)
    kv2 = move_ctx(kv, lambda i: i ^ 2)
    kv1 = move_ctx(kv, lambda i: i ^ 1)

    head_ids = jnp.arange(H, dtype=jnp.int32)
    onehot = (routes[:, :, None] == head_ids[None, None, :]).astype(F32)
    per_token = jnp.sum(onehot, axis=1)
    below = (jnp.arange(32)[:, None] > jnp.arange(32)[None, :]).astype(F32)
    earlier = jnp.dot(below, per_token, preferred_element_type=F32)
    ranking = jnp.sum(onehot * earlier[:, None, :], axis=2).astype(jnp.int32)
    target = (routes * CAP + ranking).T.reshape(1, 512)
    gate_row = gates.T.reshape(1, 512)
    packed = pl.pallas_call(
        pack_kernel,
        out_shape=jax.ShapeDtypeStruct((16, 80, HD), BF),
        in_specs=[vmem()] * 3,
        out_specs=vmem(),
        compiler_params=grant(12),
        name="pack",
    )(queries, target, gate_row)
    arrived = lax.all_to_all(packed, "head", split_axis=0, concat_axis=0, tiled=True)
    q_own = arrived[:, :64, :]
    meta = arrived[:, 64:68, :64].astype(F32).reshape(16, 4, 4, CAP).transpose(1, 2, 0, 3).reshape(4, 4, 256)
    tok = meta[0] - 1.0
    gate = meta[1] + meta[2] + meta[3]
    dev = (jnp.arange(256) // CAP).astype(F32)
    in_block = jnp.maximum(tok, 0.0) + (dev[None, :] % 4.0) * 32.0

    a_id = jnp.arange(64)
    usable = (block_mask == 1) & (a_id[None, :] < a_id[:, None])
    usable = lax.dynamic_index_in_dim(usable.reshape(NX, NJ, 4, NX, NJ, 4), j, 1, keepdims=False)
    usable = lax.dynamic_index_in_dim(usable, x, 2, keepdims=False)
    usable = jnp.stack([lax.dynamic_index_in_dim(usable, j ^ i, 2, keepdims=False) for i in range(4)], axis=2)
    usable = jnp.stack([lax.dynamic_index_in_dim(usable, (x + dx) % NX, 0, keepdims=False) for dx in range(4)])
    flags = jnp.any(usable, axis=1).astype(jnp.int32).reshape(4, 16)
    bias = jnp.where(usable, 0.0, 2.0 * NEG).reshape(4, 4, 16).transpose(0, 2, 1)
    bias = jnp.concatenate([bias, jnp.full((4, 8, 4), 2.0 * NEG, F32)], axis=1)
    bias = jnp.repeat(bias, 64, axis=2).reshape(96, 256)
    same = (jnp.arange(256)[None, :] // 64) == jnp.arange(4)[:, None]
    earlier_ok = jnp.where(bias[0:4] == 0.0, 127.0, -1.0)
    lim = jnp.where(same[None], in_block[:, None, :], earlier_ok[None]).reshape(16, 256)

    q1 = move_ctx(q_own, lambda i: (i - 4) % 16)
    q2 = move_ctx(q_own, lambda i: (i - 8) % 16)
    q3 = move_ctx(q_own, lambda i: (i - 12) % 16)
    kv3 = move_ctx(kv2, lambda i: i ^ 1)
    kvs = (kv, kv1, kv2, kv3)
    parts = attend((1, 2, 3), flags, bias, lim, (q1, q2, q3), kvs)
    back = [move_ctx(part, lambda i: (i + 4 * dx) % 16) for dx, part in ((1, parts[0]), (2, parts[1]), (3, parts[2]))]
    (own,) = attend((0,), flags, bias, lim, (q_own,), kvs)
    sent = pl.pallas_call(
        merge_kernel,
        out_shape=jax.ShapeDtypeStruct((528, 256), BF),
        in_specs=[vmem()] * 6,
        out_specs=vmem(),
        compiler_params=grant(8),
        name="merge",
    )(own, *back, tok, gate)
    got = move_head(sent, swap)
    w_swapped = [move_ctx(w, lambda i: i ^ 1) for w in w_fetched]
    mine = own_product(jnp.stack([y, ctx % 2]), sent, w_out)

    def shift(step):
        return lambda i: (i // NZ) * NZ + (i % NZ + step) % NZ

    here, there = [], []
    for chunk, hops in ((0, (4, 3)), (1, (3, 4))):
        where = jnp.stack([y, ctx % 2, (z + hops[0]) % NZ, (z - hops[1]) % NZ])
        product, *first = with_partner(where, chunk, got, mine, w_fetched[chunk], w_swapped[chunk])
        product = product.reshape(2, NZ, 32, HALF)

        def term(dest, product=product):
            return lax.dynamic_index_in_dim(product, dest % NZ, 1, keepdims=False)

        total = term(z).astype(F32)
        for step, length, message in zip((1, -1), hops, first):
            for hop in range(length):
                if hop:
                    message = (message.astype(F32) + term(z + step * (length - hop)).astype(F32)).astype(BF)
                message = move_head(message, shift(step))
            total = total + message.astype(F32)
        total = total.astype(BF)
        here.append(lax.dynamic_index_in_dim(total, y, 0, keepdims=False))
        there.append(move_head(lax.dynamic_index_in_dim(total, 1 - y, 0, keepdims=False), swap))
    low = [jnp.where(y == 0, h, t) for h, t in zip(here, there)]
    high = [jnp.where(y == 0, t, h) for h, t in zip(here, there)]
    return jnp.concatenate(low + high, axis=1)


def solution(mesh):
    placed = (
        P(("ctx", "head"), None),
        P("ctx", "head"),
        P("ctx", "head"),
        P(("ctx", "head"), None),
        P(("ctx", "head"), None),
        P(),
        P("head", None),
    )
    return jax.shard_map(layer, mesh=mesh, in_specs=placed, out_specs=P(("ctx", "head"), None), check_vma=False)
```

time: 528 us -> 196 us (0.37)
  waiting for transfers between devices: 222 us -> 82.3 us
  matrix products: 98.9 us -> 0.12 us
  blocking collectives: 78 us -> 0 us
  local copies, waits for them, and re-layouts: 60.5 us -> 10.5 us
  starting transfers between devices: 11.2 us -> 56.9 us
  Pallas kernels: 0 us -> 33.1 us
  other arithmetic: 41.5 us -> 8.84 us
  between operations: 13.6 us -> 0.48 us
    reduce_scatter x1 -> x0, waiting for transfers between devices: 222 us -> none  [local(): lax.psum_scatter(jnp.dot(weighted, w_out, preferred_element_type=jnp.floa...]
    dot_general x35 -> x1, matrix products: 98.9 us -> 0.12 us  [layer(): earlier = jnp.dot(below, per_token, preferred_element_type=F32)]
    all_gather x2 -> x0, blocking collectives: 78 us -> none  [the longest x1 41.7 us: local(): lax.all_gather(gates, 'head', axis=0, tiled=True)]
    ppermute x0 -> x30, waiting for transfers between devices: none -> 73.2 us  [the longest x19 55.3 us: move_head(): return lax.ppermute(v, 'head', [(i, f(i)) for i in range(16)])]
    ppermute x0 -> x30, starting transfers between devices: none -> 45.9 us  [the longest x19 30.8 us: move_head(): return lax.ppermute(v, 'head', [(i, f(i)) for i in range(16)])]
    gather x17 -> x0, local copies, waits for them, and re-layouts: 44.1 us -> none  [the longest x16 41.1 us: update(): jnp.take(query_rows, key_pos // BLK, axis=2)]
    reduce_sum x22 -> x2, other arithmetic: 37 us -> 0.4 us  [the longest x1 0.24 us: layer(): ranking = jnp.sum(onehot * earlier[:, None, :], axis=2).astype(jnp.int32)]
    pallas_call x0 -> x7, Pallas kernels: none -> 33.1 us  [the longest x2 12.6 us: with_partner(): pl.pallas_call(partner_kernel, out_shape=[jax.ShapeDtypeStruct((512, HALF...]
  transfers between devices with their start and end apart: 3 -> 31, of which waited for: 1 -> 16; matrix products, arithmetic and copies ran while one was open for 8% -> 8% of each run, Pallas kernels for 0% -> 17%
where the time goes in v1:
time: 196 us; the launch traced here: 192 us
  waiting for transfers between devices  82.3 us (42%)
  starting transfers between devices  56.9 us (29%)
  Pallas kernels  33.1 us (17%)
  local copies, waits for them, and re-layouts  10.5 us (5%)
  other arithmetic  8.84 us (5%)
    ppermute x19, waiting for transfers between devices, move_head(): return lax.ppermute(v, 'head', [(i, f(i)) for i in range(16)])  55.3 us
    ppermute x19, starting transfers between devices, move_head(): return lax.ppermute(v, 'head', [(i, f(i)) for i in range(16)])  30.8 us
    ppermute x11, waiting for transfers between devices, move_ctx(): return lax.ppermute(v, 'ctx', [(i, f(i)) for i in range(16)])  17.9 us
    ppermute x11, starting transfers between devices, move_ctx(): return lax.ppermute(v, 'ctx', [(i, f(i)) for i in range(16)])  15.1 us
    pallas_call x2, Pallas kernels, with_partner(): pl.pallas_call(partner_kernel, out_shape=[jax.ShapeDtypeStruct((512, HALF...  12.6 us
    all_to_all x1, starting transfers between devices, layer(): lax.all_to_all(packed, 'head', split_axis=0, concat_axis=0, tiled=True)  10.9 us
    pallas_call x1, Pallas kernels, own_product(): pl.pallas_call(own_kernel, out_shape=jax.ShapeDtypeStruct((512, 2 * HALF)...  9.2 us
    all_to_all x1, waiting for transfers between devices, layer(): lax.all_to_all(packed, 'head', split_axis=0, concat_axis=0, tiled=True)  9.06 us
  transfers between devices with their start and end apart: 31, of which 16 were waited for; matrix products, arithmetic and copies ran while one was open for 8% of the time, Pallas kernels for 17%

profile of v1, /device:TPU:4, one launch (start us, length us, event | category | flops | bytes accessed | tf_op | source)
XLA Modules:
  0.0 192.2 jit_solution(4224275747806258710)
XLA Ops:
  2.4 1.7 collective-permute-start.1
  6.4 10.9 %all-to-all-start = ((bf16[16,80,128]{2,1,0:T(8,128)(2,1)}), bf16[16,80,128]{2,1,0:T(8,128)(2,1)}, u32[]{:S(2)}, u32[]{:S(2)}) async-start(bf16[16,80,128]{2,1,0:T(8,128)(2,1)} %pack.1), calls=%async_computation | async-start | bytes 655360 | tf_op jit(solution)/shard_map/all_to_all | solution.py:331
  17.4 3.2 %fusion.21 = (bf16[256,2048]{1,0:T(8,128)(2,1)}, bf16[256,2048]{1,0:T(8,128)(2,1)}) fusion(bf16[512,8192]{1,0:T(8,128)(2,1)} %w_ref.1, s32[]{:T(128)S(6)} %select_n.276, s32[]{:T(128)S(6)} %select_n.277, s32[]{:T(128)S(6)} %add.379), kind=kLoop, calls=%fused_computation.83 | loop fusion | bytes 4194316 | tf_op jit(solution)/shard_map/slice | solution.py:309
  20.6 3.3 %collective-permute-start.10 = (bf16[256,2048]{1,0:T(8,128)(2,1)}, bf16[256,2048]{1,0:T(8,128)(2,1)}, u32[]{:S(2)}, u32[]{:S(2)}) collective-permute-start(bf16[256,2048]{1,0:T(8,128)(2,1)} %get-tuple-element.23), channel_id=1, source_target_pairs={{0,128},{16,144},{32,160},{48,176},{64,192},{80,208},{96,224},{112... | collective-permute-start | bytes 3145736 | tf_op jit(solution)/shard_map/ppermute | solution.py:303
  25.5 9.1 %all-to-all-done = bf16[16,80,128]{2,1,0:T(8,128)(2,1)} async-done(((bf16[16,80,128]{2,1,0:T(8,128)(2,1)}), bf16[16,80,128]{2,1,0:T(8,128)(2,1)}, u32[]{:S(2)}, u32[]{:S(2)}) %all-to-all-start) | async-done | bytes 327712 | tf_op jit(solution)/shard_map/all_to_all | solution.py:331
  37.0 5.2 %collective-permute-done.3.refs_3_ = bf16[16,64,128]{2,1,0:T(8,128)(2,1)} collective-permute-done((bf16[16,64,128]{2,1,0:T(8,128)(2,1)S(1)}, bf16[16,64,128]{2,1,0:T(8,128)(2,1)}, u32[]{:S(2)}, u32[]{:S(2)}) %collective-permute-start.3) | collective-permute-done | bytes 262176 | tf_op jit(solution)/shard_map/ppermute | solution.py:300
  46.0 5.5 %collective-permute-done.4.refs_4_ = bf16[16,64,128]{2,1,0:T(8,128)(2,1)} collective-permute-done((bf16[16,64,128]{2,1,0:T(8,128)(2,1)S(1)}, bf16[16,64,128]{2,1,0:T(8,128)(2,1)}, u32[]{:S(2)}, u32[]{:S(2)}) %collective-permute-start.4) | collective-permute-done | bytes 262176 | tf_op jit(solution)/shard_map/ppermute | solution.py:300
  53.2 3.9 %collective-permute-done.10.wb_ref = bf16[256,2048]{1,0:T(8,128)(2,1)} collective-permute-done((bf16[256,2048]{1,0:T(8,128)(2,1)}, bf16[256,2048]{1,0:T(8,128)(2,1)}, u32[]{:S(2)}, u32[]{:S(2)}) %collective-permute-start.10) | collective-permute-done | bytes 1048608 | tf_op jit(solution)/shard_map/ppermute | solution.py:303
  57.1 21.3 %collective-permute-done.20.wb_ref = bf16[256,2048]{1,0:T(8,128)(2,1)} collective-permute-done((bf16[256,2048]{1,0:T(8,128)(2,1)}, bf16[256,2048]{1,0:T(8,128)(2,1)}, u32[]{:S(2)}, u32[]{:S(2)}) %collective-permute-start.20) | collective-permute-done | bytes 1048608 | tf_op jit(solution)/shard_map/ppermute | solution.py:303
  78.4 6.2 %attend.3 = (bf16[528,256]{1,0:T(8,128)(2,1)}, bf16[528,256]{1,0:T(8,128)(2,1)}, bf16[528,256]{1,0:T(8,128)(2,1)}) custom-call(s32[4,16]{1,0:T(4,128)S(1)} %reshape.186.refs_0_, f32[96,256]{1,0:T(8,128)S(1)} %reshape_reshape.3.refs_1_, f32[16,256]{1,0:T(8,128)S(1)} %select_n.275.refs_2_, bf16[16,64,128]{2,1,0:T(8,128)(2,1)} %collective-permute-done.3.refs_3_, ...), custom_call_target="tpu_custom_call" | custom-call | flops 3221225472 | bytes 5242880 | tf_op jit(solution)/shard_map/attend/pallas_call | solution.py:157
  84.7 8.7 %collective-permute-start.7 = (bf16[528,256]{1,0:T(8,128)(2,1)}, bf16[528,256]{1,0:T(8,128)(2,1)}, u32[]{:S(2)}, u32[]{:S(2)}) collective-permute-start(bf16[528,256]{1,0:T(8,128)(2,1)} %get-tuple-element.15), channel_id=1, source_target_pairs={{0,8},{1,9},{2,10},{3,11},{4,12},{5,13},{6,14},{7,15},{8,0},{9,1},... | collective-permute-start | bytes 811016 | tf_op jit(solution)/shard_map/ppermute | solution.py:300
  93.4 2.3 %collective-permute-start.8 = (bf16[528,256]{1,0:T(8,128)(2,1)}, bf16[528,256]{1,0:T(8,128)(2,1)}, u32[]{:S(2)}, u32[]{:S(2)}) collective-permute-start(bf16[528,256]{1,0:T(8,128)(2,1)} %get-tuple-element.16), channel_id=1, source_target_pairs={{0,12},{1,13},{2,14},{3,15},{4,0},{5,1},{6,2},{7,3},{8,4},{9,5},{1... | collective-permute-start | bytes 811016 | tf_op jit(solution)/shard_map/ppermute | solution.py:300
  97.2 2.4 %attend.2.a_ref = bf16[528,256]{1,0:T(8,128)(2,1)S(1)} custom-call(s32[4,16]{1,0:T(4,128)S(1)} %reshape.186.refs_0_, f32[96,256]{1,0:T(8,128)S(1)} %reshape_reshape.3.refs_1_, f32[16,256]{1,0:T(8,128)S(1)} %select_n.275.refs_2_, bf16[16,64,128]{2,1,0:T(8,128)(2,1)S(1)} %slice.43.refs_3_, bf16[1024,512]{1,0:T(8,128)(2,1)S(1)} %pad_maximum_fusion.refs_4_.refs_6_, ...), custom_call_target="tpu_custom_call" | custom-call | flops 1073741824 | bytes 5242880 | tf_op jit(solution)/shard_map/attend/pallas_call | solution.py:157
  99.7 5.7 %collective-permute-done.7.c_ref = bf16[528,256]{1,0:T(8,128)(2,1)} collective-permute-done((bf16[528,256]{1,0:T(8,128)(2,1)}, bf16[528,256]{1,0:T(8,128)(2,1)}, u32[]{:S(2)}, u32[]{:S(2)}) %collective-permute-start.7) | collective-permute-done | bytes 270368 | tf_op jit(solution)/shard_map/ppermute | solution.py:300
  109.5 9.2 %own_product.1.own_ref = bf16[512,4096]{1,0:T(8,128)(2,1)} custom-call(s32[2]{0:T(128)} %pad_add_fusion.3.place_ref, bf16[528,256]{1,0:T(8,128)(2,1)} %copy-done, bf16[512,8192]{1,0:T(8,128)(2,1)} %w_ref.1), custom_call_target="tpu_custom_call" | custom-call | flops 2147483648 | bytes 8388608 | tf_op jit(solution)/shard_map/own_product/pallas_call | solution.py:252
  119.7 6.3 %with_partner.2 = (bf16[512,2048]{1,0:T(8,128)(2,1)}, bf16[2,32,2048]{2,1,0:T(8,128)(2,1)}, bf16[2,32,2048]{2,1,0:T(8,128)(2,1)}) custom-call(s32[4]{0:T(128)} %pad_add_fusion.1.place_ref, bf16[528,256]{1,0:T(8,128)(2,1)} %copy-done.4, bf16[512,4096]{1,0:T(8,128)(2,1)} %own_product.1.own_ref, bf16[256,2048]{1,0:T(8,128)(2,1)} %collective-permute-done.10.wb_ref, ...), custom_call_target="tpu_custom_call" | custom-call | flops 1073741824 | bytes 6291456 | tf_op jit(solution)/shard_map/with_partner/pallas_call | solution.py:272
  126.0 1.9 %collective-permute-start.12 = (bf16[2,32,2048]{2,1,0:T(8,128)(2,1)}, bf16[2,32,2048]{2,1,0:T(8,128)(2,1)S(1)}, u32[]{:S(2)}, u32[]{:S(2)}) collective-permute-start(bf16[2,32,2048]{2,1,0:T(8,128)(2,1)} %get-tuple-element.18), channel_id=1, source_target_pairs={{0,16},{16,32},{32,48},{48,64},{64,80},{80,96},{96,112},{112,0},{1... | collective-permute-start | bytes 786440 | tf_op jit(solution)/shard_map/ppermute | solution.py:303
  128.5 4.1 %collective-permute-start.16 = (bf16[2,32,2048]{2,1,0:T(8,128)(2,1)}, bf16[2,32,2048]{2,1,0:T(8,128)(2,1)S(1)}, u32[]{:S(2)}, u32[]{:S(2)}) collective-permute-start(bf16[2,32,2048]{2,1,0:T(8,128)(2,1)} %get-tuple-element.19), channel_id=1, source_target_pairs={{0,112},{16,0},{32,16},{48,32},{64,48},{80,64},{96,80},{112,96},{1... | collective-permute-start | bytes 786440 | tf_op jit(solution)/shard_map/ppermute | solution.py:303
  132.6 6.3 %with_partner.3 = (bf16[512,2048]{1,0:T(8,128)(2,1)}, bf16[2,32,2048]{2,1,0:T(8,128)(2,1)}, bf16[2,32,2048]{2,1,0:T(8,128)(2,1)}) custom-call(s32[4]{0:T(128)} %pad_add_fusion.4.place_ref, bf16[528,256]{1,0:T(8,128)(2,1)} %copy-done.4, bf16[512,4096]{1,0:T(8,128)(2,1)} %own_product.1.own_ref, bf16[256,2048]{1,0:T(8,128)(2,1)} %collective-permute-done.20.wb_ref, ...), custom_call_target="tpu_custom_call" | custom-call | flops 1073741824 | bytes 6291456 | tf_op jit(solution)/shard_map/with_partner/pallas_call | solution.py:272
  138.9 3.2 %collective-permute-start.25 = (bf16[2,32,2048]{2,1,0:T(8,128)(2,1)}, bf16[2,32,2048]{2,1,0:T(8,128)(2,1)S(1)}, u32[]{:S(2)}, u32[]{:S(2)}) collective-permute-start(bf16[2,32,2048]{2,1,0:T(8,128)(2,1)} %get-tuple-element.22), channel_id=1, source_target_pairs={{0,112},{16,0},{32,16},{48,32},{64,48},{80,64},{96,80},{112,96},{1... | collective-permute-start | bytes 786440 | tf_op jit(solution)/shard_map/ppermute | solution.py:303
  142.3 7.2 %collective-permute-done.22 = bf16[2,32,2048]{2,1,0:T(8,128)(2,1)S(1)} collective-permute-done((bf16[2,32,2048]{2,1,0:T(8,128)(2,1)}, bf16[2,32,2048]{2,1,0:T(8,128)(2,1)S(1)}, u32[]{:S(2)}, u32[]{:S(2)}) %collective-permute-start.22) | collective-permute-done | bytes 262176 | tf_op jit(solution)/shard_map/ppermute | solution.py:303
  150.8 3.2 %collective-permute-start.26 = (bf16[2,32,2048]{2,1,0:T(8,128)(2,1)S(1)}, bf16[2,32,2048]{2,1,0:T(8,128)(2,1)S(1)}, u32[]{:S(2)}, u32[]{:S(2)}) collective-permute-start(bf16[2,32,2048]{2,1,0:T(8,128)(2,1)S(1)} %get-tuple-element.30), channel_id=1, source_target_pairs={{0,112},{16,0},{32,16},{48,32},{64,48},{80,64},{96,80},{112,96},{1... | collective-permute-start | bytes 786440 | tf_op jit(solution)/shard_map/ppermute | solution.py:303
  155.3 5.9 %collective-permute-done.23 = bf16[2,32,2048]{2,1,0:T(8,128)(2,1)S(1)} collective-permute-done((bf16[2,32,2048]{2,1,0:T(8,128)(2,1)S(1)}, bf16[2,32,2048]{2,1,0:T(8,128)(2,1)S(1)}, u32[]{:S(2)}, u32[]{:S(2)}) %collective-permute-start.23) | collective-permute-done | bytes 262176 | tf_op jit(solution)/shard_map/ppermute | solution.py:303
  163.4 3.4 %collective-permute-done.14 = bf16[2,32,2048]{2,1,0:T(8,128)(2,1)S(1)} collective-permute-done((bf16[2,32,2048]{2,1,0:T(8,128)(2,1)S(1)}, bf16[2,32,2048]{2,1,0:T(8,128)(2,1)S(1)}, u32[]{:S(2)}, u32[]{:S(2)}) %collective-permute-start.14) | collective-permute-done | bytes 262176 | tf_op jit(solution)/shard_map/ppermute | solution.py:303
  169.1 2.1 %collective-permute-start.28 = (bf16[2,32,2048]{2,1,0:T(8,128)(2,1)S(1)}, bf16[2,32,2048]{2,1,0:T(8,128)(2,1)S(1)}, u32[]{:S(2)}, u32[]{:S(2)}) collective-permute-start(bf16[2,32,2048]{2,1,0:T(8,128)(2,1)S(1)} %fusion), channel_id=1, source_target_pairs={{0,112},{16,0},{32,16},{48,32},{64,48},{80,64},{96,80},{112,96},{1... | collective-permute-start | bytes 786440 | tf_op jit(solution)/shard_map/ppermute | solution.py:303
  171.2 5.0 %collective-permute-done.17 = bf16[2,32,2048]{2,1,0:T(8,128)(2,1)S(1)} collective-permute-done((bf16[2,32,2048]{2,1,0:T(8,128)(2,1)S(1)}, bf16[2,32,2048]{2,1,0:T(8,128)(2,1)S(1)}, u32[]{:S(2)}, u32[]{:S(2)}) %collective-permute-start.17) | collective-permute-done | bytes 262176 | tf_op jit(solution)/shard_map/ppermute | solution.py:303
  176.2 2.1 %collective-permute-start.18 = (bf16[2,32,2048]{2,1,0:T(8,128)(2,1)S(1)}, bf16[2,32,2048]{2,1,0:T(8,128)(2,1)S(1)}, u32[]{:S(2)}, u32[]{:S(2)}) collective-permute-start(bf16[2,32,2048]{2,1,0:T(8,128)(2,1)S(1)} %fusion.7), channel_id=1, source_target_pairs={{0,112},{16,0},{32,16},{48,32},{64,48},{80,64},{96,80},{112,96},{1... | collective-permute-start | bytes 786440 | tf_op jit(solution)/shard_map/ppermute | solution.py:303
  178.3 3.5 %collective-permute-done.28 = bf16[2,32,2048]{2,1,0:T(8,128)(2,1)S(1)} collective-permute-done((bf16[2,32,2048]{2,1,0:T(8,128)(2,1)S(1)}, bf16[2,32,2048]{2,1,0:T(8,128)(2,1)S(1)}, u32[]{:S(2)}, u32[]{:S(2)}) %collective-permute-start.28) | collective-permute-done | bytes 262176 | tf_op jit(solution)/shard_map/ppermute | solution.py:303
  181.9 2.8 %collective-permute-start.29 = (bf16[32,2048]{1,0:T(8,128)(2,1)S(1)}, bf16[32,2048]{1,0:T(8,128)(2,1)S(1)}, u32[]{:S(2)}, u32[]{:S(2)}) collective-permute-start(bf16[32,2048]{1,0:T(8,128)(2,1)S(1)} %dynamic-slice_bitcast_fusion), channel_id=1, source_target_pairs={{0,128},{16,144},{32,160},{48,176},{64,192},{80,208},{96,224},{112... | collective-permute-start | bytes 393224 | tf_op jit(solution)/shard_map/ppermute | solution.py:303
  184.8 2.7 %collective-permute-start.19 = (bf16[32,2048]{1,0:T(8,128)(2,1)S(1)}, bf16[32,2048]{1,0:T(8,128)(2,1)S(1)}, u32[]{:S(2)}, u32[]{:S(2)}) collective-permute-start(bf16[32,2048]{1,0:T(8,128)(2,1)S(1)} %dynamic-slice_bitcast_fusion.1), channel_id=1, source_target_pairs={{0,128},{16,144},{32,160},{48,176},{64,192},{80,208},{96,224},{112... | collective-permute-start | bytes 393224 | tf_op jit(solution)/shard_map/ppermute | solution.py:303
  187.5 1.5 collective-permute-done.29
  189.1 2.3 %collective-permute-done.19 = bf16[32,2048]{1,0:T(8,128)(2,1)S(1)} collective-permute-done((bf16[32,2048]{1,0:T(8,128)(2,1)S(1)}, bf16[32,2048]{1,0:T(8,128)(2,1)S(1)}, u32[]{:S(2)}, u32[]{:S(2)}) %collective-permute-start.19) | collective-permute-done | bytes 131104 | tf_op jit(solution)/shard_map/ppermute | solution.py:303
  (119 shorter events, 29.8 us)
Async XLA Ops:
  2.4 33.8 %collective-permute-start.1 = (bf16[1024,512]{1,0:T(8,128)(2,1)S(1)}, bf16[1024,512]{1,0:T(8,128)(2,1)S(1)}, u32[]{:S(2)}, u32[]{:S(2)}) collective-permute-start(bf16[1024,512]{1,0:T(8,128)(2,1)S(1)} %pad_maximum_fusion.refs_4_.refs_6_), channel_id=1, source_target_pairs={{0,2},{1,3},{2,0},{3,1},{4,6},{5,7},{6,4},{7,5},{8,10},{9,11},{10,... | collective-permute-start | bytes 3145736 | tf_op jit(solution)/shard_map/ppermute | solution.py:300
  4.1 74.3 %collective-permute-start = (bf16[1024,512]{1,0:T(8,128)(2,1)S(1)}, bf16[1024,512]{1,0:T(8,128)(2,1)S(1)}, u32[]{:S(2)}, u32[]{:S(2)}) collective-permute-start(bf16[1024,512]{1,0:T(8,128)(2,1)S(1)} %pad_maximum_fusion.refs_4_.refs_6_), channel_id=1, source_target_pairs={{0,1},{1,0},{2,3},{3,2},{4,5},{5,4},{6,7},{7,6},{8,9},{9,8},{10,11... | collective-permute-start | bytes 3145736 | tf_op jit(solution)/shard_map/ppermute | solution.py:300
  6.4 28.2 %all-to-all-start = ((bf16[16,80,128]{2,1,0:T(8,128)(2,1)}), bf16[16,80,128]{2,1,0:T(8,128)(2,1)}, u32[]{:S(2)}, u32[]{:S(2)}) async-start(bf16[16,80,128]{2,1,0:T(8,128)(2,1)} %pack.1), calls=%async_computation | async-start | bytes 655360 | tf_op jit(solution)/shard_map/all_to_all | solution.py:331
  20.6 36.5 %collective-permute-start.10 = (bf16[256,2048]{1,0:T(8,128)(2,1)}, bf16[256,2048]{1,0:T(8,128)(2,1)}, u32[]{:S(2)}, u32[]{:S(2)}) collective-permute-start(bf16[256,2048]{1,0:T(8,128)(2,1)} %get-tuple-element.23), channel_id=1, source_target_pairs={{0,128},{16,144},{32,160},{48,176},{64,192},{80,208},{96,224},{112... | collective-permute-start | bytes 3145736 | tf_op jit(solution)/shard_map/ppermute | solution.py:303
  23.9 54.5 %collective-permute-start.20 = (bf16[256,2048]{1,0:T(8,128)(2,1)}, bf16[256,2048]{1,0:T(8,128)(2,1)}, u32[]{:S(2)}, u32[]{:S(2)}) collective-permute-start(bf16[256,2048]{1,0:T(8,128)(2,1)} %get-tuple-element.24), channel_id=1, source_target_pairs={{0,128},{16,144},{32,160},{48,176},{64,192},{80,208},{96,224},{112... | collective-permute-start | bytes 3145736 | tf_op jit(solution)/shard_map/ppermute | solution.py:303
  35.6 6.6 %collective-permute-start.3 = (bf16[16,64,128]{2,1,0:T(8,128)(2,1)S(1)}, bf16[16,64,128]{2,1,0:T(8,128)(2,1)}, u32[]{:S(2)}, u32[]{:S(2)}) collective-permute-start(bf16[16,64,128]{2,1,0:T(8,128)(2,1)S(1)} %slice.43.refs_3_), channel_id=1, source_target_pairs={{0,12},{1,13},{2,14},{3,15},{4,0},{5,1},{6,2},{7,3},{8,4},{9,5},{1... | collective-permute-start | bytes 786440 | tf_op jit(solution)/shard_map/ppermute | solution.py:300
  36.2 42.2 %collective-permute-start.2 = (bf16[1024,512]{1,0:T(8,128)(2,1)S(1)}, bf16[1024,512]{1,0:T(8,128)(2,1)}, u32[]{:S(2)}, u32[]{:S(2)}) collective-permute-start(bf16[1024,512]{1,0:T(8,128)(2,1)S(1)} %collective-permute-done.1.refs_6_.refs_8_), channel_id=1, source_target_pairs={{0,1},{1,0},{2,3},{3,2},{4,5},{5,4},{6,7},{7,6},{8,9},{9,8},{10,11... | collective-permute-start | bytes 3145736 | tf_op jit(solution)/shard_map/ppermute | solution.py:300
  42.1 9.4 %collective-permute-start.4 = (bf16[16,64,128]{2,1,0:T(8,128)(2,1)S(1)}, bf16[16,64,128]{2,1,0:T(8,128)(2,1)}, u32[]{:S(2)}, u32[]{:S(2)}) collective-permute-start(bf16[16,64,128]{2,1,0:T(8,128)(2,1)S(1)} %slice.43.refs_3_), channel_id=1, source_target_pairs={{0,8},{1,9},{2,10},{3,11},{4,12},{5,13},{6,14},{7,15},{8,0},{9,1},... | collective-permute-start | bytes 786440 | tf_op jit(solution)/shard_map/ppermute | solution.py:300
  51.5 26.9 %collective-permute-start.5 = (bf16[16,64,128]{2,1,0:T(8,128)(2,1)S(1)}, bf16[16,64,128]{2,1,0:T(8,128)(2,1)}, u32[]{:S(2)}, u32[]{:S(2)}) collective-permute-start(bf16[16,64,128]{2,1,0:T(8,128)(2,1)S(1)} %slice.43.refs_3_), channel_id=1, source_target_pairs={{0,4},{1,5},{2,6},{3,7},{4,8},{5,9},{6,10},{7,11},{8,12},{9,13},{1... | collective-permute-start | bytes 786440 | tf_op jit(solution)/shard_map/ppermute | solution.py:300
  57.1 61.7 %collective-permute-start.11 = (bf16[256,2048]{1,0:T(8,128)(2,1)}, bf16[256,2048]{1,0:T(8,128)(2,1)}, u32[]{:S(2)}, u32[]{:S(2)}) collective-permute-start(bf16[256,2048]{1,0:T(8,128)(2,1)} %collective-permute-done.10.wb_ref), channel_id=1, source_target_pairs={{0,1},{1,0},{2,3},{3,2},{4,5},{5,4},{6,7},{7,6},{8,9},{9,8},{10,11... | collective-permute-start | bytes 3145736 | tf_op jit(solution)/shard_map/ppermute | solution.py:300
  78.4 54.2 %collective-permute-start.21 = (bf16[256,2048]{1,0:T(8,128)(2,1)}, bf16[256,2048]{1,0:T(8,128)(2,1)}, u32[]{:S(2)}, u32[]{:S(2)}) collective-permute-start(bf16[256,2048]{1,0:T(8,128)(2,1)} %collective-permute-done.20.wb_ref), channel_id=1, source_target_pairs={{0,1},{1,0},{2,3},{3,2},{4,5},{5,4},{6,7},{7,6},{8,9},{9,8},{10,11... | collective-permute-start | bytes 3145736 | tf_op jit(solution)/shard_map/ppermute | solution.py:300
  84.6 15.0 %collective-permute-start.6 = (bf16[528,256]{1,0:T(8,128)(2,1)}, bf16[528,256]{1,0:T(8,128)(2,1)}, u32[]{:S(2)}, u32[]{:S(2)}) collective-permute-start(bf16[528,256]{1,0:T(8,128)(2,1)} %get-tuple-element.14), channel_id=1, source_target_pairs={{0,4},{1,5},{2,6},{3,7},{4,8},{5,9},{6,10},{7,11},{8,12},{9,13},{1... | collective-permute-start | bytes 811016 | tf_op jit(solution)/shard_map/ppermute | solution.py:300
  84.7 20.6 %collective-permute-start.7 = (bf16[528,256]{1,0:T(8,128)(2,1)}, bf16[528,256]{1,0:T(8,128)(2,1)}, u32[]{:S(2)}, u32[]{:S(2)}) collective-permute-start(bf16[528,256]{1,0:T(8,128)(2,1)} %get-tuple-element.15), channel_id=1, source_target_pairs={{0,8},{1,9},{2,10},{3,11},{4,12},{5,13},{6,14},{7,15},{8,0},{9,1},... | collective-permute-start | bytes 811016 | tf_op jit(solution)/shard_map/ppermute | solution.py:300
  93.4 13.4 %collective-permute-start.8 = (bf16[528,256]{1,0:T(8,128)(2,1)}, bf16[528,256]{1,0:T(8,128)(2,1)}, u32[]{:S(2)}, u32[]{:S(2)}) collective-permute-start(bf16[528,256]{1,0:T(8,128)(2,1)} %get-tuple-element.16), channel_id=1, source_target_pairs={{0,12},{1,13},{2,14},{3,15},{4,0},{5,1},{6,2},{7,3},{8,4},{9,5},{1... | collective-permute-start | bytes 811016 | tf_op jit(solution)/shard_map/ppermute | solution.py:300
  108.2 10.8 %collective-permute-start.9 = (bf16[528,256]{1,0:T(8,128)(2,1)S(1)}, bf16[528,256]{1,0:T(8,128)(2,1)S(1)}, u32[]{:S(2)}, u32[]{:S(2)}) collective-permute-start(bf16[528,256]{1,0:T(8,128)(2,1)S(1)} %merge.1.sent_ref), channel_id=1, source_target_pairs={{0,128},{16,144},{32,160},{48,176},{64,192},{80,208},{96,224},{112... | collective-permute-start | bytes 811016 | tf_op jit(solution)/shard_map/ppermute | solution.py:303
  126.0 16.2 %collective-permute-start.12 = (bf16[2,32,2048]{2,1,0:T(8,128)(2,1)}, bf16[2,32,2048]{2,1,0:T(8,128)(2,1)S(1)}, u32[]{:S(2)}, u32[]{:S(2)}) collective-permute-start(bf16[2,32,2048]{2,1,0:T(8,128)(2,1)} %get-tuple-element.18), channel_id=1, source_target_pairs={{0,16},{16,32},{32,48},{48,64},{64,80},{80,96},{96,112},{112,0},{1... | collective-permute-start | bytes 786440 | tf_op jit(solution)/shard_map/ppermute | solution.py:303
  128.5 34.9 %collective-permute-start.16 = (bf16[2,32,2048]{2,1,0:T(8,128)(2,1)}, bf16[2,32,2048]{2,1,0:T(8,128)(2,1)S(1)}, u32[]{:S(2)}, u32[]{:S(2)}) collective-permute-start(bf16[2,32,2048]{2,1,0:T(8,128)(2,1)} %get-tuple-element.19), channel_id=1, source_target_pairs={{0,112},{16,0},{32,16},{48,32},{64,48},{80,64},{96,80},{112,96},{1... | collective-permute-start | bytes 786440 | tf_op jit(solution)/shard_map/ppermute | solution.py:303
  138.9 22.3 %copy-start.3 = (bf16[512,2048]{1,0:T(8,128)(2,1)S(1)}, bf16[512,2048]{1,0:T(8,128)(2,1)}, u32[]{:S(2)}) copy-start(bf16[512,2048]{1,0:T(8,128)(2,1)} %get-tuple-element.20) | copy-start | bytes 6291460
  138.9 10.7 %collective-permute-start.22 = (bf16[2,32,2048]{2,1,0:T(8,128)(2,1)}, bf16[2,32,2048]{2,1,0:T(8,128)(2,1)S(1)}, u32[]{:S(2)}, u32[]{:S(2)}) collective-permute-start(bf16[2,32,2048]{2,1,0:T(8,128)(2,1)} %get-tuple-element.21), channel_id=1, source_target_pairs={{0,16},{16,32},{32,48},{48,64},{64,80},{80,96},{96,112},{112,0},{1... | collective-permute-start | bytes 786440 | tf_op jit(solution)/shard_map/ppermute | solution.py:303
  138.9 10.6 %collective-permute-start.25 = (bf16[2,32,2048]{2,1,0:T(8,128)(2,1)}, bf16[2,32,2048]{2,1,0:T(8,128)(2,1)S(1)}, u32[]{:S(2)}, u32[]{:S(2)}) collective-permute-start(bf16[2,32,2048]{2,1,0:T(8,128)(2,1)} %get-tuple-element.22), channel_id=1, source_target_pairs={{0,112},{16,0},{32,16},{48,32},{64,48},{80,64},{96,80},{112,96},{1... | collective-permute-start | bytes 786440 | tf_op jit(solution)/shard_map/ppermute | solution.py:303
  142.2 12.9 %collective-permute-start.13 = (bf16[2,32,2048]{2,1,0:T(8,128)(2,1)S(1)}, bf16[2,32,2048]{2,1,0:T(8,128)(2,1)S(1)}, u32[]{:S(2)}, u32[]{:S(2)}) collective-permute-start(bf16[2,32,2048]{2,1,0:T(8,128)(2,1)S(1)} %fusion.11), channel_id=1, source_target_pairs={{0,16},{16,32},{32,48},{48,64},{64,80},{80,96},{96,112},{112,0},{1... | collective-permute-start | bytes 786440 | tf_op jit(solution)/shard_map/ppermute | solution.py:303
  150.7 10.5 %collective-permute-start.23 = (bf16[2,32,2048]{2,1,0:T(8,128)(2,1)S(1)}, bf16[2,32,2048]{2,1,0:T(8,128)(2,1)S(1)}, u32[]{:S(2)}, u32[]{:S(2)}) collective-permute-start(bf16[2,32,2048]{2,1,0:T(8,128)(2,1)S(1)} %get-tuple-element.29), channel_id=1, source_target_pairs={{0,16},{16,32},{32,48},{48,64},{64,80},{80,96},{96,112},{112,0},{1... | collective-permute-start | bytes 786440 | tf_op jit(solution)/shard_map/ppermute | solution.py:303
  150.8 10.4 %collective-permute-start.26 = (bf16[2,32,2048]{2,1,0:T(8,128)(2,1)S(1)}, bf16[2,32,2048]{2,1,0:T(8,128)(2,1)S(1)}, u32[]{:S(2)}, u32[]{:S(2)}) collective-permute-start(bf16[2,32,2048]{2,1,0:T(8,128)(2,1)S(1)} %get-tuple-element.30), channel_id=1, source_target_pairs={{0,112},{16,0},{32,16},{48,32},{64,48},{80,64},{96,80},{112,96},{1... | collective-permute-start | bytes 786440 | tf_op jit(solution)/shard_map/ppermute | solution.py:303
  155.2 11.6 %collective-permute-start.14 = (bf16[2,32,2048]{2,1,0:T(8,128)(2,1)S(1)}, bf16[2,32,2048]{2,1,0:T(8,128)(2,1)S(1)}, u32[]{:S(2)}, u32[]{:S(2)}) collective-permute-start(bf16[2,32,2048]{2,1,0:T(8,128)(2,1)S(1)} %fusion.10), channel_id=1, source_target_pairs={{0,16},{16,32},{32,48},{48,64},{64,80},{80,96},{96,112},{112,0},{1... | collective-permute-start | bytes 786440 | tf_op jit(solution)/shard_map/ppermute | solution.py:303
  161.3 7.7 %collective-permute-start.27 = (bf16[2,32,2048]{2,1,0:T(8,128)(2,1)S(1)}, bf16[2,32,2048]{2,1,0:T(8,128)(2,1)S(1)}, u32[]{:S(2)}, u32[]{:S(2)}) collective-permute-start(bf16[2,32,2048]{2,1,0:T(8,128)(2,1)S(1)} %get-tuple-element.28), channel_id=1, source_target_pairs={{0,112},{16,0},{32,16},{48,32},{64,48},{80,64},{96,80},{112,96},{1... | collective-permute-start | bytes 786440 | tf_op jit(solution)/shard_map/ppermute | solution.py:303
  162.2 16.1 %collective-permute-start.24 = (bf16[2,32,2048]{2,1,0:T(8,128)(2,1)S(1)}, bf16[2,32,2048]{2,1,0:T(8,128)(2,1)S(1)}, u32[]{:S(2)}, u32[]{:S(2)}) collective-permute-start(bf16[2,32,2048]{2,1,0:T(8,128)(2,1)S(1)} %get-tuple-element.27), channel_id=1, source_target_pairs={{0,16},{16,32},{32,48},{48,64},{64,80},{80,96},{96,112},{112,0},{1... | collective-permute-start | bytes 786440 | tf_op jit(solution)/shard_map/ppermute | solution.py:303
  166.9 9.3 %collective-permute-start.17 = (bf16[2,32,2048]{2,1,0:T(8,128)(2,1)S(1)}, bf16[2,32,2048]{2,1,0:T(8,128)(2,1)S(1)}, u32[]{:S(2)}, u32[]{:S(2)}) collective-permute-start(bf16[2,32,2048]{2,1,0:T(8,128)(2,1)S(1)} %get-tuple-element.26), channel_id=1, source_target_pairs={{0,112},{16,0},{32,16},{48,32},{64,48},{80,64},{96,80},{112,96},{1... | collective-permute-start | bytes 786440 | tf_op jit(solution)/shard_map/ppermute | solution.py:303
  167.8 16.9 %collective-permute-start.15 = (bf16[2,32,2048]{2,1,0:T(8,128)(2,1)S(1)}, bf16[2,32,2048]{2,1,0:T(8,128)(2,1)S(1)}, u32[]{:S(2)}, u32[]{:S(2)}) collective-permute-start(bf16[2,32,2048]{2,1,0:T(8,128)(2,1)S(1)} %get-tuple-element.25), channel_id=1, source_target_pairs={{0,16},{16,32},{32,48},{48,64},{64,80},{80,96},{96,112},{112,0},{1... | collective-permute-start | bytes 786440 | tf_op jit(solution)/shard_map/ppermute | solution.py:303
  169.1 12.7 %collective-permute-start.28 = (bf16[2,32,2048]{2,1,0:T(8,128)(2,1)S(1)}, bf16[2,32,2048]{2,1,0:T(8,128)(2,1)S(1)}, u32[]{:S(2)}, u32[]{:S(2)}) collective-permute-start(bf16[2,32,2048]{2,1,0:T(8,128)(2,1)S(1)} %fusion), channel_id=1, source_target_pairs={{0,112},{16,0},{32,16},{48,32},{64,48},{80,64},{96,80},{112,96},{1... | collective-permute-start | bytes 786440 | tf_op jit(solution)/shard_map/ppermute | solution.py:303
  176.2 8.4 %collective-permute-start.18 = (bf16[2,32,2048]{2,1,0:T(8,128)(2,1)S(1)}, bf16[2,32,2048]{2,1,0:T(8,128)(2,1)S(1)}, u32[]{:S(2)}, u32[]{:S(2)}) collective-permute-start(bf16[2,32,2048]{2,1,0:T(8,128)(2,1)S(1)} %fusion.7), channel_id=1, source_target_pairs={{0,112},{16,0},{32,16},{48,32},{64,48},{80,64},{96,80},{112,96},{1... | collective-permute-start | bytes 786440 | tf_op jit(solution)/shard_map/ppermute | solution.py:303
  181.9 7.1 %collective-permute-start.29 = (bf16[32,2048]{1,0:T(8,128)(2,1)S(1)}, bf16[32,2048]{1,0:T(8,128)(2,1)S(1)}, u32[]{:S(2)}, u32[]{:S(2)}) collective-permute-start(bf16[32,2048]{1,0:T(8,128)(2,1)S(1)} %dynamic-slice_bitcast_fusion), channel_id=1, source_target_pairs={{0,128},{16,144},{32,160},{48,176},{64,192},{80,208},{96,224},{112... | collective-permute-start | bytes 393224 | tf_op jit(solution)/shard_map/ppermute | solution.py:303
  184.8 6.6 %collective-permute-start.19 = (bf16[32,2048]{1,0:T(8,128)(2,1)S(1)}, bf16[32,2048]{1,0:T(8,128)(2,1)S(1)}, u32[]{:S(2)}, u32[]{:S(2)}) collective-permute-start(bf16[32,2048]{1,0:T(8,128)(2,1)S(1)} %dynamic-slice_bitcast_fusion.1), channel_id=1, source_target_pairs={{0,128},{16,144},{32,160},{48,176},{64,192},{80,208},{96,224},{112... | collective-permute-start | bytes 393224 | tf_op jit(solution)/shard_map/ppermute | solution.py:303
  (7 other events, 36.4 us)
